TPU v7x, 32 devices: a whole 2x2x4 slice. The times are simulated.
32 devices in a mesh: sn: 8 (over y, x, core), blk: 4 (over z).
Axes of the slice: x: 2, y: 2, z: 4, core: 2. Of those that a mesh axis runs over, the one named last changes fastest.
Arguments:
- root_inverse: float32 [2048, 2048], P('sn'), as said below
- structure: int32 [8, 4], replicated, may hold values from 0 to 7, as said below
- panel_one: float32 [8, 1024, 256], P('sn', 'blk'), may hold values from -0.375 to 0.375
- inverse_one: float32 [8, 256, 256], P('sn'), as said below
- parent_two: float32 [8, 256, 256], P('sn'), may hold values from -0.375 to 0.375
- panel_two: float32 [8, 1024, 256], P('sn', 'blk'), may hold values from -0.375 to 0.375
- inverse_two: float32 [8, 256, 256], P('sn'), as said below
Outputs:
- sigma_diag_one: float32 [8, 256, 256], P('sn')
- sigma_off_one: float32 [8, 1024, 256], P('sn', 'blk')
- sigma_diag_two: float32 [8, 256, 256], P('sn')
- sigma_par_two: float32 [8, 256, 256], P('sn')
- sigma_root_two: float32 [8, 1024, 256], P('sn', 'blk')
Inputs may be any that keep to these rules, and one draw needn't show every extreme that they name: `structure`: each row holds 4 distinct block indices. `inverse_one`: lower triangular; diagonal between 0.5 and 1.5. `inverse_two`: lower triangular; diagonal between 0.5 and 1.5. `root_inverse`: Symmetric.
All inputs are finite; a program needn't handle non-finite values.
Results may differ from a plain program's by a relative error of at most 0.00011.
Values sent between devices are 32-bit elements; how exact they have to be, the bound alone decides.
No kernel may reach another device: no remote copies, remote signals or barrier semaphores. Data moves between devices by JAX's collectives and lax.ppermute only.
A program may use at most 128 MiB of HBM per device.

v0:
```python
import jax
import jax.numpy as jnp
from jax import lax
from jax.sharding import PartitionSpec as P


def product(left, right):
    return jnp.dot(left, right, precision=lax.Precision.HIGHEST, preferred_element_type=jnp.float32)


def per_device(root_inverse, structure, panel_one, inverse_one, parent_two, panel_two, inverse_two):
    width = inverse_one.shape[-1]
    groups = lax.axis_size("blk")
    per_group = structure.shape[1] // groups
    owner = lax.axis_index("sn")
    position_group = lax.axis_index("blk")
    inv_one = inverse_one[0]
    inv_two = inverse_two[0]
    u_one = product(panel_one[0], inv_one)
    u_root = product(panel_two[0], inv_two)
    u_par = product(parent_two[0], inv_two)
    stacked = jnp.concatenate([u_one, u_root], axis=1)
    group_lists = lax.dynamic_slice_in_dim(structure, position_group * per_group, per_group, 1)
    block_count = root_inverse.shape[1] // width
    local_rows = root_inverse.reshape(root_inverse.shape[0], block_count, width)
    listed_cols = jnp.take(local_rows, structure, axis=1)
    listed_cols = listed_cols.reshape(
        local_rows.shape[0], structure.shape[0], structure.shape[1] * width
    )
    listed_cols = jnp.transpose(listed_cols, (1, 0, 2))
    named = (group_lists == owner).astype(jnp.float32)
    outgoing = named[:, :, None, None] * listed_cols[:, None, :, :]
    incoming = lax.all_to_all(outgoing, "sn", split_axis=0, concat_axis=0, tiled=True)
    own_rows = jnp.sum(incoming, axis=0).reshape(per_group * width, structure.shape[1] * width)
    full_panels = lax.all_gather(stacked, "blk", axis=0, tiled=True)
    combined = product(own_rows, full_panels)
    w_one = combined[:, :width]
    w_two = combined[:, width:]
    off_one = -w_one
    square_one = product(inv_one.T, inv_one)
    square_two = product(inv_two.T, inv_two)
    diag_term = product(u_one.T, w_one)
    root_two = -(w_two + product(off_one, u_par))
    child_term = product(u_root.T, root_two)
    diag_one = square_one + lax.psum(diag_term, "blk")
    parent_total, child_total = lax.psum((product(off_one.T, u_root), child_term), "blk")
    par_two = -(parent_total + product(diag_one, u_par))
    diag_two = square_two - product(u_par.T, par_two) - child_total
    return (diag_one[None], off_one[None], diag_two[None], par_two[None], root_two[None])


def solution(mesh):
    return jax.shard_map(
        per_device,
        mesh=mesh,
        in_specs=(
            P("sn", None),
            P(),
            P("sn", "blk", None),
            P("sn", None, None),
            P("sn", None, None),
            P("sn", "blk", None),
            P("sn", None, None),
        ),
        out_specs=(
            P("sn", None, None),
            P("sn", "blk", None),
            P("sn", None, None),
            P("sn", None, None),
            P("sn", "blk", None),
        ),
        check_vma=False,
    )
```

profile of v0, /device:TPU:0, one launch (start us, length us, event | category | flops | bytes accessed | tf_op | source)
XLA Modules:
  0.0 204.8 jit_solution(13430769693259133787)
XLA Ops:
  7.2 0.0 copy-start
  7.2 0.7 compare_select_fusion
  7.9 0.7 compare_and_fusion
  8.6 2.9 %copy.18 = f32[256,2048]{0,1:T(8,128)} copy(f32[256,2048]{1,0:T(8,128)} %param.7) | data formatting | bytes 4194304 | tf_op args[0]
  11.5 1.9 copy.20
  13.4 0.1 copy.19
  13.5 0.1 reshape.33
  13.6 4.3 %gather_fusion = f32[32,256,256]{2,1,0:T(8,128)} fusion(f32[256,8,256]{2,0,1:T(8,128)S(1)} %copy.20, s32[1024]{0:T(1024)S(1)} %pad_clamp_fusion), kind=kCustom, calls=%fused_computation | custom fusion | bytes 16777344 | tf_op jit(solution)/shard_map/jit(_take)/gather | solution.py:26
  17.9 9.2 %copy.21 = f32[8,4,256,256]{2,3,1,0:T(8,128)} copy(f32[8,4,256,256]{3,2,1,0:T(8,128)} %bitcast.57) | data formatting | bytes 16777216 | tf_op jit(solution)/shard_map/jit(_take)/gather | solution.py:26
  27.1 0.7 fusion.21
  27.8 0.1 broadcast_in_dim.33
  27.8 7.4 %fusion = f32[256,8,1024]{0,2,1:T(8,128)} fusion(f32[8,4,256,256]{2,3,1,0:T(8,128)} %copy.21, f32[8]{0:T(128)S(1)} %fusion.21, pred[8,1024]{1,0:T(8,128)(4,1)S(1)} %bitcast.63), kind=kLoop, calls=%fused_computation.2 | loop fusion | flops 4194304 | bytes 16785440 | tf_op jit(solution)/shard_map/mul | solution.py:32
  35.3 0.0 copy-start.5
  35.3 0.0 copy-start.1
  35.3 5.3 %all-to-all-start = ((f32[8,1,256,1024]{2,3,1,0:T(8,128)}), f32[8,1,256,1024]{2,3,1,0:T(8,128)}, u32[]{:S(2)}, u32[]{:S(2)}) async-start(f32[8,1,256,1024]{2,3,1,0:T(8,128)} %bitcast.58), calls=%async_computation | async-start | bytes 16777216 | tf_op jit(solution)/shard_map/all_to_all | solution.py:33
  40.6 0.0 all-gather.2.cloned.1.call-start
  40.7 0.0 copy-done
  40.7 0.0 copy-done.5
  40.7 0.6 fusion.10
  41.3 0.0 copy-done.1
  41.3 0.0 copy-done.6
  41.3 0.6 fusion.13
  41.9 0.8 pad_maximum_fusion
  42.8 0.0 all-gather.2.cloned.1.call-update
  42.8 0.2 all-reduce.3.cloned.1.call-start
  43.0 0.0 copy-done.7
  43.0 0.4 fusion.5
  43.4 91.7 %all-to-all-done = f32[8,1,256,1024]{2,3,1,0:T(8,128)} async-done(((f32[8,1,256,1024]{2,3,1,0:T(8,128)}), f32[8,1,256,1024]{2,3,1,0:T(8,128)}, u32[]{:S(2)}, u32[]{:S(2)}) %all-to-all-start) | async-done | bytes 8388640 | tf_op jit(solution)/shard_map/all_to_all | solution.py:33
  135.1 4.1 %bitcast_reduce_fusion = f32[256,1024]{0,1:T(8,128)S(1)} fusion(f32[8,1,256,1024]{2,3,1,0:T(8,128)} %all-to-all-done), kind=kLoop, calls=%fused_computation.3 | loop fusion | flops 1835008 | bytes 9437184 | tf_op jit(solution)/shard_map/reduce_sum | solution.py:34
  139.2 0.0 all-gather.2.cloned.1.call-done
  139.2 5.1 %fusion.22 = f32[256,512]{1,0:T(8,128)S(1)} fusion(f32[256,1024]{0,1:T(8,128)S(1)} %bitcast_reduce_fusion, f32[1024,512]{0,1:T(8,128)} %all-gather.2.cloned.1.call-done), kind=kOutput, calls=%fused_computation.35 | convolution fusion | flops 1610612736 | bytes 3670016 | tf_op jit(solution)/shard_map/dot_general | solution.py:8
  144.3 1.3 fusion.19
  145.6 1.1 fusion.17
  146.7 0.4 fusion.1
  147.1 0.0 copy-start.2
  147.1 1.1 fusion.23
  148.2 0.0 all-reduce.3.cloned.1.call-update
  148.2 0.6 fusion.8
  148.8 0.7 fusion.20
  149.6 43.0 %all-reduce.3.cloned.1.call-done = (f32[256,256]{1,0:T(8,128)}, f32[256,256]{1,0:T(8,128)}, f32[256,256]{1,0:T(8,128)}) async-done(((f32[256,256]{1,0:T(8,128)}, f32[256,256]{1,0:T(8,128)}, f32[256,256]{1,0:T(8,128)}), (f32[256,256]{1,0:T(8,128)}, f32[256,256]{1,0:T(8,128)}, f32[256,256]{1,0:T(8,128)})) %all-reduce.3.cloned.1.call-update) | async-done | bytes 786448 | tf_op jit(solution)/shard_map/psum | solution.py:45
  192.6 1.5 convolution_add_fusion.2
  194.1 0.0 copy-start.3
  194.2 1.4 fusion.4
  195.6 0.0 copy-start.4
  195.6 2.4 %fusion.3 = f32[1,256,256]{2,1,0:T(8,128)} fusion(f32[256,256]{1,0:T(8,128)} %get-tuple-element.6, f32[256,256]{1,0:T(8,128)S(1)} %fusion.8, f32[256,256]{1,0:T(8,128)S(1)} %fusion.5, f32[256,256]{1,0:T(8,128)S(1)} %fusion.4), kind=kOutput, calls=%fused_computation.8 | convolution fusion | flops 201457664 | bytes 1310720 | tf_op jit(solution)/shard_map/dot_general | solution.py:8
  197.9 0.0 copy-done.2
  197.9 0.0 copy-done.3
  198.0 0.0 copy-done.4
  (3 shorter events, 0.0 us)
Async XLA Ops:
  7.2 33.5 %copy-start = (f32[1,256,256]{2,1,0:T(8,128)S(1)}, f32[1,256,256]{2,1,0:T(8,128)}, u32[]{:S(2)}) copy-start(f32[1,256,256]{2,1,0:T(8,128)} %param.13) | copy-start | bytes 786436
  35.3 5.4 %copy-start.5 = (f32[1,256,256]{2,1,0:T(8,128)S(1)}, f32[1,256,256]{2,1,0:T(8,128)}, u32[]{:S(2)}) copy-start(f32[1,256,256]{2,1,0:T(8,128)} %param.12) | copy-start | bytes 786436
  35.3 6.0 %copy-start.1 = (f32[1,256,256]{2,1,0:T(8,128)S(1)}, f32[1,256,256]{2,1,0:T(8,128)}, u32[]{:S(2)}) copy-start(f32[1,256,256]{2,1,0:T(8,128)} %param.10) | copy-start | bytes 786436
  35.3 6.0 %copy-start.6 = (f32[1,256,256]{2,1,0:T(8,128)S(1)}, f32[1,256,256]{2,1,0:T(8,128)}, u32[]{:S(2)}) copy-start(f32[1,256,256]{2,1,0:T(8,128)} %param.9) | copy-start | bytes 786436
  35.3 7.7 %copy-start.7 = (f32[1,256,256]{2,1,0:T(8,128)S(1)}, f32[1,256,256]{2,1,0:T(8,128)}, u32[]{:S(2)}) copy-start(f32[1,256,256]{2,1,0:T(8,128)} %param.11) | copy-start | bytes 786436
  35.3 99.8 %all-to-all-start = ((f32[8,1,256,1024]{2,3,1,0:T(8,128)}), f32[8,1,256,1024]{2,3,1,0:T(8,128)}, u32[]{:S(2)}, u32[]{:S(2)}) async-start(f32[8,1,256,1024]{2,3,1,0:T(8,128)} %bitcast.58), calls=%async_computation | async-start | bytes 16777216 | tf_op jit(solution)/shard_map/all_to_all | solution.py:33
  40.6 98.6 %all-gather.2.cloned.1.call-start = ((), (), s32[]{:S(2)}) async-start(), calls=%async_computation.1 | async-start | bytes 2621440 | tf_op jit(solution)/shard_map/all_gather | solution.py:35
  42.8 149.8 %all-reduce.3.cloned.1.call-start = ((), (), s32[]{:S(2)}) async-start(), calls=%async_computation.2 | async-start | bytes 1572864 | tf_op jit(solution)/shard_map/psum | solution.py:45
  147.1 50.8 %copy-start.2 = (f32[256,256]{1,0:T(8,128)}, f32[256,256]{1,0:T(8,128)S(1)}, u32[]{:S(2)}) copy-start(f32[256,256]{1,0:T(8,128)S(1)} %fusion.1) | copy-start | bytes 786436
  194.1 3.8 %copy-start.3 = (f32[256,256]{1,0:T(8,128)}, f32[256,256]{1,0:T(8,128)S(1)}, u32[]{:S(2)}) copy-start(f32[256,256]{1,0:T(8,128)S(1)} %convolution_add_fusion.2) | copy-start | bytes 786436
  195.6 2.4 %copy-start.4 = (f32[256,256]{1,0:T(8,128)}, f32[256,256]{1,0:T(8,128)S(1)}, u32[]{:S(2)}) copy-start(f32[256,256]{1,0:T(8,128)S(1)} %fusion.4) | copy-start | bytes 786436
Sparse Core Ops, SparseCore 0:
  43.0 48.5 all-gather.1
  148.3 44.1 all-reduce.2
where the time goes:
time: 205 us
  waiting for transfers between devices  135 us (66%)
  local copies, waits for them, and re-layouts  18.6 us (9%)
  matrix products  16.4 us (8%)
  other arithmetic  15.2 us (7%)
  between operations  14.2 us (7%)
  starting transfers between devices  5.6 us (3%)
    all_to_all x1, waiting for transfers between devices, per_device(): lax.all_to_all(outgoing, 'sn', split_axis=0, concat_axis=0, tiled=True)  91.7 us
    psum x1, waiting for transfers between devices, per_device(): diag_one = square_one + lax.psum(diag_term, 'blk')  43 us
    dot_general x12, matrix products, product(): jnp.dot(left, right, precision=lax.Precision.HIGHEST, preferred_element_t...  16.4 us
    gather x2, local copies, waits for them, and re-layouts, per_device(): listed_cols = jnp.take(local_rows, structure, axis=1)  13.5 us
    mul x2, other arithmetic, per_device(): outgoing = named[:, :, None, None] * listed_cols[:, None, :, :]  8.12 us
    all_to_all x1, starting transfers between devices, per_device(): lax.all_to_all(outgoing, 'sn', split_axis=0, concat_axis=0, tiled=True)  5.34 us
  transfers between devices with their start and end apart: 3, of which 2 were waited for; matrix products, arithmetic and copies ran while one was open for 4% of the time, Pallas kernels for 0%

commit v1 on v0

--- a/solution.py
+++ b/solution.py
@@ -42,7 +42,7 @@
     diag_term = product(u_one.T, w_one)
     root_two = -(w_two + product(off_one, u_par))
     child_term = product(u_root.T, root_two)
-    diag_one = square_one + lax.psum(diag_term, "blk")
+    diag_one = square_one + jnp.sum(lax.all_gather(diag_term, "blk"), 0)
     parent_total, child_total = lax.psum((product(off_one.T, u_root), child_term), "blk")
     par_two = -(parent_total + product(diag_one, u_par))
     diag_two = square_two - product(u_par.T, par_two) - child_total

time: 205 us -> 226 us (1.10)
  waiting for transfers between devices: 135 us -> 155 us
    all_gather x0 -> x1, waiting for transfers between devices: none -> 23.6 us  [per_device(): diag_one = square_one + jnp.sum(lax.all_gather(diag_term, 'blk'), 0)]
    psum x1, waiting for transfers between devices: 43 us -> 39.1 us  [per_device(): lax.psum((product(off_one.T, u_root), child_term), 'blk')]
  transfers between devices with their start and end apart: 3 -> 4, of which waited for: 2 -> 3; matrix products, arithmetic and copies ran while one was open for 4% -> 6% of each run, Pallas kernels for 0% -> 0%
where the time goes in v1:
time: 226 us; the launch traced here: 225 us
  waiting for transfers between devices  155 us (69%)
  local copies, waits for them, and re-layouts  18.6 us (8%)
  other arithmetic  16.5 us (7%)
  matrix products  15.4 us (7%)
  between operations  13.9 us (6%)
  starting transfers between devices  5.64 us (2%)
    all_to_all x1, waiting for transfers between devices, per_device(): lax.all_to_all(outgoing, 'sn', split_axis=0, concat_axis=0, tiled=True)  92.3 us
    psum x1, waiting for transfers between devices, per_device(): lax.psum((product(off_one.T, u_root), child_term), 'blk')  39.1 us
    all_gather x1, waiting for transfers between devices, per_device(): diag_one = square_one + jnp.sum(lax.all_gather(diag_term, 'blk'), 0)  23.6 us
    dot_general x12, matrix products, product(): jnp.dot(left, right, precision=lax.Precision.HIGHEST, preferred_element_t...  15.4 us
    gather x2, local copies, waits for them, and re-layouts, per_device(): listed_cols = jnp.take(local_rows, structure, axis=1)  13.5 us
    mul x2, other arithmetic, per_device(): outgoing = named[:, :, None, None] * listed_cols[:, None, :, :]  8.12 us
    all_to_all x1, starting transfers between devices, per_device(): lax.all_to_all(outgoing, 'sn', split_axis=0, concat_axis=0, tiled=True)  5.34 us
  transfers between devices with their start and end apart: 4, of which 3 were waited for; matrix products, arithmetic and copies ran while one was open for 6% of the time, Pallas kernels for 0%

profile of v1, /device:TPU:0, one launch (start us, length us, event | category | flops | bytes accessed | tf_op | source)
XLA Modules:
  0.0 225.1 jit_solution(2383565569119919262)
XLA Ops:
  7.2 0.0 copy-start
  7.2 0.7 compare_select_fusion
  7.9 0.7 compare_and_fusion
  8.6 2.9 %copy.18 = f32[256,2048]{0,1:T(8,128)} copy(f32[256,2048]{1,0:T(8,128)} %param.7) | data formatting | bytes 4194304 | tf_op args[0]
  11.5 1.9 copy.20
  13.4 0.1 copy.19
  13.5 0.1 reshape.33
  13.6 4.3 %gather_fusion = f32[32,256,256]{2,1,0:T(8,128)} fusion(f32[256,8,256]{2,0,1:T(8,128)S(1)} %copy.20, s32[1024]{0:T(1024)S(1)} %pad_clamp_fusion), kind=kCustom, calls=%fused_computation | custom fusion | bytes 16777344 | tf_op jit(solution)/shard_map/jit(_take)/gather | solution.py:26
  17.9 9.2 %copy.21 = f32[8,4,256,256]{2,3,1,0:T(8,128)} copy(f32[8,4,256,256]{3,2,1,0:T(8,128)} %bitcast.58) | data formatting | bytes 16777216 | tf_op jit(solution)/shard_map/jit(_take)/gather | solution.py:26
  27.1 0.7 fusion.21
  27.8 0.1 broadcast_in_dim.33
  27.8 7.4 %fusion = f32[256,8,1024]{0,2,1:T(8,128)} fusion(f32[8,4,256,256]{2,3,1,0:T(8,128)} %copy.21, f32[8]{0:T(128)S(1)} %fusion.21, pred[8,1024]{1,0:T(8,128)(4,1)S(1)} %bitcast.65), kind=kLoop, calls=%fused_computation.2 | loop fusion | flops 4194304 | bytes 16785440 | tf_op jit(solution)/shard_map/mul | solution.py:32
  35.3 5.3 %all-to-all-start = ((f32[8,1,256,1024]{2,3,1,0:T(8,128)}), f32[8,1,256,1024]{2,3,1,0:T(8,128)}, u32[]{:S(2)}, u32[]{:S(2)}) async-start(f32[8,1,256,1024]{2,3,1,0:T(8,128)} %bitcast.59), calls=%async_computation | async-start | bytes 16777216 | tf_op jit(solution)/shard_map/all_to_all | solution.py:33
  40.6 0.0 all-gather.4.cloned.1.call-start
  40.7 0.0 copy-done
  40.7 0.0 copy-done.5
  40.7 0.6 fusion.10
  41.3 0.0 copy-done.1
  41.3 0.0 copy-start.7
  41.3 0.6 fusion.13
  41.9 0.8 pad_maximum_fusion
  42.8 0.0 all-gather.4.cloned.1.call-update
  42.8 0.0 all-gather.6.cloned.1.call-start
  42.8 92.3 %all-to-all-done = f32[8,1,256,1024]{2,3,1,0:T(8,128)} async-done(((f32[8,1,256,1024]{2,3,1,0:T(8,128)}), f32[8,1,256,1024]{2,3,1,0:T(8,128)}, u32[]{:S(2)}, u32[]{:S(2)}) %all-to-all-start) | async-done | bytes 8388640 | tf_op jit(solution)/shard_map/all_to_all | solution.py:33
  135.1 4.1 %bitcast_reduce_fusion = f32[256,1024]{0,1:T(8,128)S(1)} fusion(f32[8,1,256,1024]{2,3,1,0:T(8,128)} %all-to-all-done), kind=kLoop, calls=%fused_computation.3 | loop fusion | flops 1835008 | bytes 9437184 | tf_op jit(solution)/shard_map/reduce_sum | solution.py:34
  139.2 0.0 all-gather.4.cloned.1.call-done
  139.2 5.1 %fusion.22 = f32[256,512]{1,0:T(8,128)S(1)} fusion(f32[256,1024]{0,1:T(8,128)S(1)} %bitcast_reduce_fusion, f32[1024,512]{0,1:T(8,128)} %all-gather.4.cloned.1.call-done), kind=kOutput, calls=%fused_computation.35 | convolution fusion | flops 1610612736 | bytes 3670016 | tf_op jit(solution)/shard_map/dot_general | solution.py:8
  144.3 1.1 fusion.17
  145.4 0.0 all-gather.6.cloned.1.call-update
  145.4 0.2 all-reduce.3.cloned.1.call-start
  145.7 0.0 copy-done.7
  145.7 0.4 fusion.5
  146.1 1.3 fusion.19
  147.4 0.4 fusion.1
  147.8 0.0 copy-start.2
  147.8 1.1 fusion.23
  148.9 0.0 all-reduce.3.cloned.1.call-update
  148.9 0.6 fusion.8
  149.5 0.7 fusion.20
  150.2 23.6 %all-gather.6.cloned.1.call-done = f32[1024,256]{1,0:T(8,128)} async-done(((f32[256,256]{1,0:T(8,128)}), f32[1024,256]{1,0:T(8,128)}) %all-gather.6.cloned.1.call-update) | async-done | bytes 1048592 | tf_op jit(solution)/shard_map/all_gather | solution.py:45
  173.8 1.3 reduce_sum.19
  175.1 0.6 convolution_add_fusion.2
  175.7 0.0 copy-start.3
  175.7 39.1 %all-reduce.3.cloned.1.call-done = (f32[256,256]{1,0:T(8,128)}, f32[256,256]{1,0:T(8,128)}) async-done(((f32[256,256]{1,0:T(8,128)}, f32[256,256]{1,0:T(8,128)}), (f32[256,256]{1,0:T(8,128)}, f32[256,256]{1,0:T(8,128)})) %all-reduce.3.cloned.1.call-update) | async-done | bytes 524304 | tf_op jit(solution)/shard_map/psum | solution.py:46
  214.8 1.3 fusion.4
  216.1 0.0 copy-start.4
  216.2 2.3 %fusion.3 = f32[1,256,256]{2,1,0:T(8,128)} fusion(f32[256,256]{1,0:T(8,128)} %get-tuple-element.5, f32[256,256]{1,0:T(8,128)S(1)} %fusion.8, f32[256,256]{1,0:T(8,128)S(1)} %fusion.5, f32[256,256]{1,0:T(8,128)S(1)} %fusion.4), kind=kOutput, calls=%fused_computation.8 | convolution fusion | flops 201457664 | bytes 1310720 | tf_op jit(solution)/shard_map/dot_general | solution.py:8
  218.5 0.0 copy-done.4
  (7 shorter events, 0.0 us)
Async XLA Ops:
  7.2 33.5 %copy-start = (f32[1,256,256]{2,1,0:T(8,128)S(1)}, f32[1,256,256]{2,1,0:T(8,128)}, u32[]{:S(2)}) copy-start(f32[1,256,256]{2,1,0:T(8,128)} %param.13) | copy-start | bytes 786436
  35.3 5.4 %copy-start.5 = (f32[1,256,256]{2,1,0:T(8,128)S(1)}, f32[1,256,256]{2,1,0:T(8,128)}, u32[]{:S(2)}) copy-start(f32[1,256,256]{2,1,0:T(8,128)} %param.12) | copy-start | bytes 786436
  35.3 6.0 %copy-start.1 = (f32[1,256,256]{2,1,0:T(8,128)S(1)}, f32[1,256,256]{2,1,0:T(8,128)}, u32[]{:S(2)}) copy-start(f32[1,256,256]{2,1,0:T(8,128)} %param.10) | copy-start | bytes 786436
  35.3 6.0 %copy-start.6 = (f32[1,256,256]{2,1,0:T(8,128)S(1)}, f32[1,256,256]{2,1,0:T(8,128)}, u32[]{:S(2)}) copy-start(f32[1,256,256]{2,1,0:T(8,128)} %param.9) | copy-start | bytes 786436
  35.3 99.8 %all-to-all-start = ((f32[8,1,256,1024]{2,3,1,0:T(8,128)}), f32[8,1,256,1024]{2,3,1,0:T(8,128)}, u32[]{:S(2)}, u32[]{:S(2)}) async-start(f32[8,1,256,1024]{2,3,1,0:T(8,128)} %bitcast.59), calls=%async_computation | async-start | bytes 16777216 | tf_op jit(solution)/shard_map/all_to_all | solution.py:33
  40.6 98.6 %all-gather.4.cloned.1.call-start = ((), (), s32[]{:S(2)}) async-start(), calls=%async_computation.1 | async-start | bytes 2621440 | tf_op jit(solution)/shard_map/all_gather | solution.py:35
  41.3 104.4 %copy-start.7 = (f32[1,256,256]{2,1,0:T(8,128)S(1)}, f32[1,256,256]{2,1,0:T(8,128)}, u32[]{:S(2)}) copy-start(f32[1,256,256]{2,1,0:T(8,128)} %param.11) | copy-start | bytes 786436
  42.8 131.0 %all-gather.6.cloned.1.call-start = ((), (), s32[]{:S(2)}) async-start(), calls=%async_computation.2 | async-start | bytes 1310720 | tf_op jit(solution)/shard_map/all_gather | solution.py:45
  145.4 69.4 %all-reduce.3.cloned.1.call-start = ((), (), s32[]{:S(2)}) async-start(), calls=%async_computation.3 | async-start | bytes 1048576 | tf_op jit(solution)/shard_map/psum | solution.py:46
  147.8 70.8 %copy-start.2 = (f32[256,256]{1,0:T(8,128)}, f32[256,256]{1,0:T(8,128)S(1)}, u32[]{:S(2)}) copy-start(f32[256,256]{1,0:T(8,128)S(1)} %fusion.1) | copy-start | bytes 786436
  175.7 42.8 %copy-start.3 = (f32[256,256]{1,0:T(8,128)}, f32[256,256]{1,0:T(8,128)S(1)}, u32[]{:S(2)}) copy-start(f32[256,256]{1,0:T(8,128)S(1)} %convolution_add_fusion.2) | copy-start | bytes 786436
  216.1 2.4 %copy-start.4 = (f32[256,256]{1,0:T(8,128)}, f32[256,256]{1,0:T(8,128)S(1)}, u32[]{:S(2)}) copy-start(f32[256,256]{1,0:T(8,128)S(1)} %fusion.4) | copy-start | bytes 786436
Sparse Core Ops, SparseCore 0:
  43.0 48.5 all-gather.3
  145.6 28.2 all-gather.5
  176.8 37.9 all-reduce.2
